TPU v7x, 256 devices: a whole 4x4x8 slice. The times are simulated.
256 devices in a mesh: dp: 8 (over y, z_hi), tile: 32 (over x, z_lo, core).
Axes of the slice: x: 4, y: 4, z: 8 (z_hi: 2, z_lo: 4; z = z_hi * 4 + z_lo), core: 2. Of those that a mesh axis runs over, the one named last changes fastest.
Arguments:
- videos: bfloat16 [8, 32, 32, 64, 512], P('dp', 'tile'), may hold values from -6 to 6
- spatial_filter: bfloat16 [9, 512, 512], P(None, 'dp'), may hold values from -0.09375 to 0.09375
- temporal_filter: bfloat16 [3, 512, 512], P(None, 'dp'), may hold values from -0.15625 to 0.15625
- spatial_bias: float32 [512], replicated, may hold values from -3 to 3
- temporal_bias: float32 [512], replicated, may hold values from -3 to 3
Outputs:
- output: bfloat16 [8, 32, 32, 64, 512], P('dp', 'tile')
All inputs are finite; a program needn't handle non-finite values.
Results may differ from a plain program's by a relative error of at most 0.0044.
Values may be sent and summed in bfloat16 or wider, within the bound.
A program may use at most 128 MiB of HBM per device.

v0:
```python
import jax
import jax.numpy as jnp
from jax import lax
from jax.sharding import PartitionSpec as P


def padded_2(block, sides, width):
    for axis, dim in sides:
        count = lax.axis_size(axis)
        forward = [(i, i + 1) for i in range(count - 1)]
        backward = [(target, source) for source, target in forward]
        low = lax.ppermute(
            lax.slice_in_dim(block, block.shape[dim] - width, None, axis=dim), axis, forward
        )
        high = lax.ppermute(lax.slice_in_dim(block, 0, width, axis=dim), axis, backward)
        block = jnp.concatenate([low, block, high], axis=dim)
    return block


def spatial_term(padded, weight_piece):
    width = weight_piece.shape[1]
    height = padded.shape[2] - 2
    breadth = padded.shape[3] - 2
    columns = jnp.concatenate(
        [
            padded[:, :, row_off : row_off + height, col_off : col_off + breadth, :]
            for row_off in range(3)
            for col_off in range(3)
        ],
        axis=4,
    )
    matrix = weight_piece.reshape(9 * width, weight_piece.shape[2])
    return jnp.dot(columns.reshape(-1, 9 * width), matrix, preferred_element_type=jnp.float32)


def temporal_term(framed, weight_piece):
    width = weight_piece.shape[1]
    frames = framed.shape[1] - 2
    columns = jnp.concatenate([framed[:, lag : lag + frames] for lag in range(3)], axis=4)
    matrix = weight_piece.reshape(3 * width, weight_piece.shape[2])
    return jnp.dot(columns.reshape(-1, 3 * width), matrix, preferred_element_type=jnp.float32)


def per_device(videos, spatial_filter, temporal_filter, spatial_bias, temporal_bias):
    samples, frames, height, breadth, channels = videos.shape
    count_frames = videos.shape[1]
    padded = jnp.pad(videos, ((0, 0), (0, 0), (1, 1), (1, 1), (0, 0)))
    summed = spatial_term(padded, lax.all_gather(spatial_filter, "dp", axis=1, tiled=True))
    activated = jax.nn.silu(summed + spatial_bias).astype(jnp.bfloat16)
    hidden = activated.reshape(samples, count_frames, height, breadth, channels)
    framed = padded_2(hidden, (("tile", 1),), 1)
    result = temporal_term(framed, lax.all_gather(temporal_filter, "dp", axis=1, tiled=True))
    return (result + temporal_bias).astype(jnp.bfloat16).reshape(videos.shape)


def solution(mesh):
    return jax.shard_map(
        per_device,
        mesh=mesh,
        in_specs=(
            P("dp", "tile", None, None, None),
            P(None, "dp", None),
            P(None, "dp", None),
            P(),
            P(),
        ),
        out_specs=P("dp", "tile", None, None, None),
        check_vma=False,
    )
```

profile of v0, /device:TPU:1, one launch (start us, length us, event | category | flops | bytes accessed | tf_op | source)
XLA Modules:
  0.0 228.2 jit_solution(13520640981759495450)
XLA Ops:
  6.5 0.0 copy-start
  6.5 0.0 all-gather.3.cloned.1.call-start
  6.5 0.7 all-gather.3.cloned.1.call-update
  7.3 0.0 all-gather.5.cloned.1.call-start
  7.3 0.7 all-gather.5.cloned.1.call-update
  8.0 3.5 %slice_dynamic-update-slice_fusion.7 = bf16[1,1,32,64,4608]{4,3,2,1,0:T(8,128)(2,1)} fusion(bf16[1,1,32,64,512]{4,3,2,1,0:T(8,128)(2,1)} %param.5), kind=kLoop, calls=%fused_computation.15 | loop fusion | bytes 4194304
  11.5 0.0 copy-done
  11.5 1.6 slice_dynamic-update-slice_fusion.6
  13.1 2.5 %slice_dynamic-update-slice_fusion.5 = bf16[1,1,32,64,4608]{4,3,2,1,0:T(8,128)(2,1)} fusion(bf16[1,1,32,64,4608]{4,3,2,1,0:T(8,128)(2,1)} %slice_dynamic-update-slice_fusion.6, bf16[1,1,32,64,512]{4,3,2,1,0:T(8,128)(2,1)S(1)} %copy-done), kind=kLoop, calls=%fused_computation.13 | loop fusion | bytes 4194304
  15.7 2.7 %slice_dynamic-update-slice_fusion.4 = bf16[1,1,32,64,4608]{4,3,2,1,0:T(8,128)(2,1)} fusion(bf16[1,1,32,64,4608]{4,3,2,1,0:T(8,128)(2,1)} %slice_dynamic-update-slice_fusion.5, bf16[1,1,32,64,512]{4,3,2,1,0:T(8,128)(2,1)S(1)} %copy-done), kind=kLoop, calls=%fused_computation.12 | loop fusion | bytes 4194304
  18.4 1.6 constant_dynamic-update-slice_fusion
  20.0 2.5 %slice_dynamic-update-slice_fusion.3 = bf16[1,1,32,64,4608]{4,3,2,1,0:T(8,128)(2,1)} fusion(bf16[1,1,32,64,4608]{4,3,2,1,0:T(8,128)(2,1)} %constant_dynamic-update-slice_fusion, bf16[1,1,32,64,512]{4,3,2,1,0:T(8,128)(2,1)S(1)} %copy-done), kind=kLoop, calls=%fused_computation.11 | loop fusion | bytes 4194304
  22.5 2.7 %slice_dynamic-update-slice_fusion.2 = bf16[1,1,32,64,4608]{4,3,2,1,0:T(8,128)(2,1)} fusion(bf16[1,1,32,64,4608]{4,3,2,1,0:T(8,128)(2,1)} %slice_dynamic-update-slice_fusion.3, bf16[1,1,32,64,512]{4,3,2,1,0:T(8,128)(2,1)S(1)} %copy-done), kind=kLoop, calls=%fused_computation.10 | loop fusion | bytes 4194304
  25.2 0.0 copy-start.1
  25.2 1.6 slice_dynamic-update-slice_fusion.1
  26.9 2.6 %slice_dynamic-update-slice_fusion = bf16[1,1,32,64,4608]{4,3,2,1,0:T(8,128)(2,1)} fusion(bf16[1,1,32,64,4608]{4,3,2,1,0:T(8,128)(2,1)} %slice_dynamic-update-slice_fusion.1, bf16[1,1,32,64,512]{4,3,2,1,0:T(8,128)(2,1)S(1)} %copy-done), kind=kLoop, calls=%fused_computation.8 | loop fusion | bytes 4194304 | tf_op jit(solution)/shard_map/concatenate | solution.py:24
  29.4 98.5 %all-gather.3.cloned.1.call-done = bf16[9,512,512]{2,1,0:T(8,128)(2,1)} async-done(((bf16[9,64,512]{2,1,0:T(8,128)(2,1)}), bf16[9,512,512]{2,1,0:T(8,128)(2,1)}) %all-gather.3.cloned.1.call-update) | async-done | bytes 4718608 | tf_op jit(solution)/shard_map/all_gather | solution.py:48
  127.9 0.0 copy-done.1
  127.9 0.0 copy-start.2
  127.9 15.8 %multiply_convert_fusion = bf16[2048,512]{1,0:T(8,128)(2,1)S(1)} fusion(bf16[2048,4608]{1,0:T(8,128)(2,1)} %bitcast, bf16[4608,512]{1,0:T(8,128)(2,1)} %bitcast.10, f32[512]{0:T(512)S(1)} %copy-done.1), kind=kOutput, calls=%fused_computation.7 | convolution fusion | flops 9669967872 | bytes 25692160 | tf_op jit(solution)/shard_map/dot_general | solution.py:33
  143.7 3.4 %collective-permute-start = (bf16[1,1,32,64,512]{4,3,2,1,0:T(8,128)(2,1)S(1)}, bf16[1,1,32,64,512]{4,3,2,1,0:T(8,128)(2,1)}, u32[]{:S(2)}, u32[]{:S(2)}) collective-permute-start(bf16[1,1,32,64,512]{4,3,2,1,0:T(8,128)(2,1)S(1)} %bitcast.11), channel_id=1, source_target_pairs={{0,1},{1,2},{2,3},{3,4},{4,5},{5,6},{6,7},{7,8},{8,9},{9,10},{10,1... | collective-permute-start | bytes 6291464 | tf_op jit(solution)/shard_map/ppermute | solution.py:12
  147.2 2.7 %collective-permute-start.1 = (bf16[1,1,32,64,512]{4,3,2,1,0:T(8,128)(2,1)S(1)}, bf16[1,1,32,64,512]{4,3,2,1,0:T(8,128)(2,1)}, u32[]{:S(2)}, u32[]{:S(2)}) collective-permute-start(bf16[1,1,32,64,512]{4,3,2,1,0:T(8,128)(2,1)S(1)} %bitcast.12), channel_id=1, source_target_pairs={{1,0},{2,1},{3,2},{4,3},{5,4},{6,5},{7,6},{8,7},{9,8},{10,9},{11,1... | collective-permute-start | bytes 6291464 | tf_op jit(solution)/shard_map/ppermute | solution.py:15
  149.8 46.0 %all-gather.5.cloned.1.call-done = bf16[3,512,512]{2,1,0:T(8,128)(2,1)} async-done(((bf16[3,64,512]{2,1,0:T(8,128)(2,1)}), bf16[3,512,512]{2,1,0:T(8,128)(2,1)}) %all-gather.5.cloned.1.call-update) | async-done | bytes 1572880 | tf_op jit(solution)/shard_map/all_gather | solution.py:52
  195.8 0.0 collective-permute-done
  195.8 18.1 %collective-permute-done.1 = bf16[1,1,32,64,512]{4,3,2,1,0:T(8,128)(2,1)} collective-permute-done((bf16[1,1,32,64,512]{4,3,2,1,0:T(8,128)(2,1)S(1)}, bf16[1,1,32,64,512]{4,3,2,1,0:T(8,128)(2,1)}, u32[]{:S(2)}, u32[]{:S(2)}) %collective-permute-start.1) | collective-permute-done | bytes 2097184 | tf_op jit(solution)/shard_map/ppermute | solution.py:15
  213.9 0.0 copy-done.2
  214.0 7.4 %add_convert_fusion = bf16[2048,512]{1,0:T(8,128)(2,1)} fusion(bf16[1536,512]{1,0:T(8,128)(2,1)} %bitcast.13, bf16[2048,512]{1,0:T(8,128)(2,1)} %bitcast.4, bf16[2048,512]{1,0:T(8,128)(2,1)S(1)} %multiply_convert_fusion, bf16[2048,512]{1,0:T(8,128)(2,1)} %bitcast.3, f32[512]{0:T(512)S(1)} %copy-done.2), kind=kOutput, calls=%fused_computation.6 | convolution fusion | flops 3242196992 | bytes 9963520 | tf_op jit(solution)/shard_map/dot_general | solution.py:41
Async XLA Ops:
  6.5 5.0 %copy-start = (bf16[1,1,32,64,512]{4,3,2,1,0:T(8,128)(2,1)S(1)}, bf16[1,1,32,64,512]{4,3,2,1,0:T(8,128)(2,1)}, u32[]{:S(2)}) copy-start(bf16[1,1,32,64,512]{4,3,2,1,0:T(8,128)(2,1)} %param.5) | copy-start | bytes 6291460
  6.5 121.4 %all-gather.3.cloned.1.call-start = ((), (), s32[]{:S(2)}) async-start(), calls=%async_computation | async-start | bytes 5308416 | tf_op jit(solution)/shard_map/all_gather | solution.py:48
  7.3 188.5 %all-gather.5.cloned.1.call-start = ((), (), s32[]{:S(2)}) async-start(), calls=%async_computation.1 | async-start | bytes 1769472 | tf_op jit(solution)/shard_map/all_gather | solution.py:52
  25.2 102.7 %copy-start.1 = (f32[512]{0:T(512)S(1)}, f32[512]{0:T(512)}, u32[]{:S(2)}) copy-start(f32[512]{0:T(512)} %param.8) | copy-start | bytes 6148
  127.9 86.0 %copy-start.2 = (f32[512]{0:T(512)S(1)}, f32[512]{0:T(512)}, u32[]{:S(2)}) copy-start(f32[512]{0:T(512)} %param.9) | copy-start | bytes 6148
  143.7 52.1 %collective-permute-start = (bf16[1,1,32,64,512]{4,3,2,1,0:T(8,128)(2,1)S(1)}, bf16[1,1,32,64,512]{4,3,2,1,0:T(8,128)(2,1)}, u32[]{:S(2)}, u32[]{:S(2)}) collective-permute-start(bf16[1,1,32,64,512]{4,3,2,1,0:T(8,128)(2,1)S(1)} %bitcast.11), channel_id=1, source_target_pairs={{0,1},{1,2},{2,3},{3,4},{4,5},{5,6},{6,7},{7,8},{8,9},{9,10},{10,1... | collective-permute-start | bytes 6291464 | tf_op jit(solution)/shard_map/ppermute | solution.py:12
  147.2 66.8 %collective-permute-start.1 = (bf16[1,1,32,64,512]{4,3,2,1,0:T(8,128)(2,1)S(1)}, bf16[1,1,32,64,512]{4,3,2,1,0:T(8,128)(2,1)}, u32[]{:S(2)}, u32[]{:S(2)}) collective-permute-start(bf16[1,1,32,64,512]{4,3,2,1,0:T(8,128)(2,1)S(1)} %bitcast.12), channel_id=1, source_target_pairs={{1,0},{2,1},{3,2},{4,3},{5,4},{6,5},{7,6},{8,7},{9,8},{10,9},{11,1... | collective-permute-start | bytes 6291464 | tf_op jit(solution)/shard_map/ppermute | solution.py:15
Sparse Core Ops, SparseCore 0:
  10.0 117.9 all-gather.2
  130.6 65.1 all-gather.4
where the time goes:
time: 228 us
  waiting for transfers between devices  164 us (72%)
  matrix products  23.2 us (10%)
  local copies, waits for them, and re-layouts  21.4 us (9%)
  between operations  13.4 us (6%)
  starting transfers between devices  6.15 us (3%)
    all_gather x1, waiting for transfers between devices, per_device(): lax.all_gather(spatial_filter, 'dp', axis=1, tiled=True)  98.5 us
    all_gather x1, waiting for transfers between devices, per_device(): lax.all_gather(temporal_filter, 'dp', axis=1, tiled=True)  46 us
    unnamed x14, local copies, waits for them, and re-layouts  18.9 us
    ppermute x1, waiting for transfers between devices, padded_2(): lax.ppermute(lax.slice_in_dim(block, 0, width, axis=dim), axis, backward)  18.1 us
    dot_general x1, matrix products, spatial_term(): jnp.dot(columns.reshape(-1, 9 * width), matrix, preferred_element_type=jn...  15.8 us
    dot_general x1, matrix products, temporal_term(): jnp.dot(columns.reshape(-1, 3 * width), matrix, preferred_element_type=jn...  7.42 us
  transfers between devices with their start and end apart: 4, of which 3 were waited for; matrix products, arithmetic and copies ran while one was open for 16% of the time, Pallas kernels for 0%

commit v1 on v0

--- a/solution.py
+++ b/solution.py
@@ -45,7 +45,12 @@
     samples, frames, height, breadth, channels = videos.shape
     count_frames = videos.shape[1]
     padded = jnp.pad(videos, ((0, 0), (0, 0), (1, 1), (1, 1), (0, 0)))
-    summed = spatial_term(padded, lax.all_gather(spatial_filter, "dp", axis=1, tiled=True))
+    summed = spatial_term(
+        padded,
+        jnp.concatenate(
+            lax.all_to_all(jnp.stack([spatial_filter] * lax.axis_size("dp")), "dp", 0, 0), axis=1
+        ),
+    )
     activated = jax.nn.silu(summed + spatial_bias).astype(jnp.bfloat16)
     hidden = activated.reshape(samples, count_frames, height, breadth, channels)
     framed = padded_2(hidden, (("tile", 1),), 1)

time: 228 us -> 236 us (1.035)
  the two profiles are of different devices: /device:TPU:1 before, /device:TPU:29 now
where the time goes in v1:
time: 236 us; the launch traced here: 235 us
  waiting for transfers between devices  94.3 us (40%)
  starting transfers between devices  79.5 us (34%)
  local copies, waits for them, and re-layouts  26.4 us (11%)
  matrix products  21.8 us (9%)
  between operations  13.5 us (6%)
    all_to_all x1, waiting for transfers between devices, per_device(): lax.all_to_all(jnp.stack([spatial_filter] * lax.axis_size('dp')), 'dp', 0...  68.2 us
    ppermute x1, starting transfers between devices, padded_2(): lax.ppermute(lax.slice_in_dim(block, block.shape[dim] - width, None, axis...  66.5 us
    ppermute x1, waiting for transfers between devices, padded_2(): lax.ppermute(lax.slice_in_dim(block, block.shape[dim] - width, None, axis...  20.8 us
    unnamed x14, local copies, waits for them, and re-layouts  17.2 us
    dot_general x1, matrix products, spatial_term(): jnp.dot(columns.reshape(-1, 9 * width), matrix, preferred_element_type=jn...  14.3 us
    all_to_all x1, starting transfers between devices, per_device(): lax.all_to_all(jnp.stack([spatial_filter] * lax.axis_size('dp')), 'dp', 0...  10.9 us
    dot_general x1, matrix products, temporal_term(): jnp.dot(columns.reshape(-1, 3 * width), matrix, preferred_element_type=jn...  7.43 us
  transfers between devices with their start and end apart: 4, of which 3 were waited for; matrix products, arithmetic and copies ran while one was open for 16% of the time, Pallas kernels for 0%

profile of v1, /device:TPU:29, one launch (start us, length us, event | category | flops | bytes accessed | tf_op | source)
XLA Modules:
  0.0 235.3 jit_solution(7155810471273776231)
XLA Ops:
  6.5 3.9 %stack.2 = bf16[8,9,64,512]{3,2,1,0:T(8,128)(2,1)} broadcast(bf16[9,64,512]{2,1,0:T(8,128)(2,1)} %param.6), dimensions={1,2,3} | broadcast | bytes 5308416 | tf_op jit(solution)/shard_map/stack | solution.py:51
  10.4 0.0 copy-start
  10.4 10.9 %all-to-all-start = ((bf16[8,9,64,512]{3,2,1,0:T(8,128)(2,1)}), bf16[8,9,64,512]{3,2,1,0:T(8,128)(2,1)}, u32[]{:S(2)}, u32[]{:S(2)}) async-start(bf16[8,9,64,512]{3,2,1,0:T(8,128)(2,1)} %stack.2), calls=%async_computation | async-start | bytes 9437184 | tf_op jit(solution)/shard_map/all_to_all | solution.py:51
  21.3 0.0 all-gather.2.cloned.1.call-start
  21.3 0.7 all-gather.2.cloned.1.call-update
  22.0 0.0 copy-done
  22.0 2.0 slice_dynamic-update-slice_fusion.7
  24.0 1.6 slice_dynamic-update-slice_fusion.6
  25.7 2.5 %slice_dynamic-update-slice_fusion.5 = bf16[1,1,32,64,4608]{4,3,2,1,0:T(8,128)(2,1)} fusion(bf16[1,1,32,64,4608]{4,3,2,1,0:T(8,128)(2,1)} %slice_dynamic-update-slice_fusion.6, bf16[1,1,32,64,512]{4,3,2,1,0:T(8,128)(2,1)S(1)} %copy-done), kind=kLoop, calls=%fused_computation.13 | loop fusion | bytes 4194304
  28.2 2.7 %slice_dynamic-update-slice_fusion.4 = bf16[1,1,32,64,4608]{4,3,2,1,0:T(8,128)(2,1)} fusion(bf16[1,1,32,64,4608]{4,3,2,1,0:T(8,128)(2,1)} %slice_dynamic-update-slice_fusion.5, bf16[1,1,32,64,512]{4,3,2,1,0:T(8,128)(2,1)S(1)} %copy-done), kind=kLoop, calls=%fused_computation.12 | loop fusion | bytes 4194304
  30.9 1.5 constant_dynamic-update-slice_fusion
  32.4 2.6 %slice_dynamic-update-slice_fusion.3 = bf16[1,1,32,64,4608]{4,3,2,1,0:T(8,128)(2,1)} fusion(bf16[1,1,32,64,4608]{4,3,2,1,0:T(8,128)(2,1)} %constant_dynamic-update-slice_fusion, bf16[1,1,32,64,512]{4,3,2,1,0:T(8,128)(2,1)S(1)} %copy-done), kind=kLoop, calls=%fused_computation.11 | loop fusion | bytes 4194304
  35.0 2.7 %slice_dynamic-update-slice_fusion.2 = bf16[1,1,32,64,4608]{4,3,2,1,0:T(8,128)(2,1)} fusion(bf16[1,1,32,64,4608]{4,3,2,1,0:T(8,128)(2,1)} %slice_dynamic-update-slice_fusion.3, bf16[1,1,32,64,512]{4,3,2,1,0:T(8,128)(2,1)S(1)} %copy-done), kind=kLoop, calls=%fused_computation.10 | loop fusion | bytes 4194304
  37.7 1.6 slice_dynamic-update-slice_fusion.1
  39.3 2.6 %slice_dynamic-update-slice_fusion = bf16[1,1,32,64,4608]{4,3,2,1,0:T(8,128)(2,1)} fusion(bf16[1,1,32,64,4608]{4,3,2,1,0:T(8,128)(2,1)} %slice_dynamic-update-slice_fusion.1, bf16[1,1,32,64,512]{4,3,2,1,0:T(8,128)(2,1)S(1)} %copy-done), kind=kLoop, calls=%fused_computation.8 | loop fusion | bytes 4194304 | tf_op jit(solution)/shard_map/concatenate | solution.py:24
  41.8 0.0 copy-start.1
  41.8 68.2 %all-to-all-done = bf16[8,9,64,512]{3,2,1,0:T(8,128)(2,1)} async-done(((bf16[8,9,64,512]{3,2,1,0:T(8,128)(2,1)}), bf16[8,9,64,512]{3,2,1,0:T(8,128)(2,1)}, u32[]{:S(2)}, u32[]{:S(2)}) %all-to-all-start) | async-done | bytes 4718624 | tf_op jit(solution)/shard_map/all_to_all | solution.py:51
  110.1 2.7 %copy.6 = bf16[8,9,64,512]{3,2,0,1:T(8,128)(2,1)S(1)} copy(bf16[8,9,64,512]{3,2,1,0:T(8,128)(2,1)} %all-to-all-done) | data formatting | bytes 9437184 | tf_op jit(solution)/shard_map/all_to_all | solution.py:51
  112.8 0.0 copy-done.1
  112.8 0.0 copy-start.2
  112.8 14.3 %multiply_convert_fusion = bf16[2048,512]{1,0:T(8,128)(2,1)S(1)} fusion(bf16[2048,4608]{1,0:T(8,128)(2,1)} %bitcast, bf16[4608,512]{1,0:T(8,128)(2,1)S(1)} %bitcast.12, f32[512]{0:T(512)S(1)} %copy-done.1), kind=kOutput, calls=%fused_computation.7 | convolution fusion | flops 9669967872 | bytes 25692160 | tf_op jit(solution)/shard_map/dot_general | solution.py:33
  127.1 66.5 %collective-permute-start = (bf16[1,1,32,64,512]{4,3,2,1,0:T(8,128)(2,1)S(1)}, bf16[1,1,32,64,512]{4,3,2,1,0:T(8,128)(2,1)}, u32[]{:S(2)}, u32[]{:S(2)}) collective-permute-start(bf16[1,1,32,64,512]{4,3,2,1,0:T(8,128)(2,1)S(1)} %bitcast.13), channel_id=1, source_target_pairs={{0,1},{1,2},{2,3},{3,4},{4,5},{5,6},{6,7},{7,8},{8,9},{9,10},{10,1... | collective-permute-start | bytes 6291464 | tf_op jit(solution)/shard_map/ppermute | solution.py:12
  193.6 2.1 collective-permute-start.1
  195.7 0.0 all-gather.2.cloned.1.call-done
  195.7 20.8 %collective-permute-done = bf16[1,1,32,64,512]{4,3,2,1,0:T(8,128)(2,1)} collective-permute-done((bf16[1,1,32,64,512]{4,3,2,1,0:T(8,128)(2,1)S(1)}, bf16[1,1,32,64,512]{4,3,2,1,0:T(8,128)(2,1)}, u32[]{:S(2)}, u32[]{:S(2)}) %collective-permute-start) | collective-permute-done | bytes 2097184 | tf_op jit(solution)/shard_map/ppermute | solution.py:12
  216.6 4.5 %collective-permute-done.1 = bf16[1,1,32,64,512]{4,3,2,1,0:T(8,128)(2,1)} collective-permute-done((bf16[1,1,32,64,512]{4,3,2,1,0:T(8,128)(2,1)S(1)}, bf16[1,1,32,64,512]{4,3,2,1,0:T(8,128)(2,1)}, u32[]{:S(2)}, u32[]{:S(2)}) %collective-permute-start.1) | collective-permute-done | bytes 2097184 | tf_op jit(solution)/shard_map/ppermute | solution.py:15
  221.1 0.0 copy-done.2
  221.1 7.4 %add_convert_fusion = bf16[2048,512]{1,0:T(8,128)(2,1)} fusion(bf16[1536,512]{1,0:T(8,128)(2,1)} %bitcast.15, bf16[2048,512]{1,0:T(8,128)(2,1)} %bitcast.5, bf16[2048,512]{1,0:T(8,128)(2,1)S(1)} %multiply_convert_fusion, bf16[2048,512]{1,0:T(8,128)(2,1)} %bitcast.4, f32[512]{0:T(512)S(1)} %copy-done.2), kind=kOutput, calls=%fused_computation.6 | convolution fusion | flops 3242196992 | bytes 9963520 | tf_op jit(solution)/shard_map/dot_general | solution.py:41
Async XLA Ops:
  10.4 11.6 %copy-start = (bf16[1,1,32,64,512]{4,3,2,1,0:T(8,128)(2,1)S(1)}, bf16[1,1,32,64,512]{4,3,2,1,0:T(8,128)(2,1)}, u32[]{:S(2)}) copy-start(bf16[1,1,32,64,512]{4,3,2,1,0:T(8,128)(2,1)} %param.5) | copy-start | bytes 6291460
  10.4 99.7 %all-to-all-start = ((bf16[8,9,64,512]{3,2,1,0:T(8,128)(2,1)}), bf16[8,9,64,512]{3,2,1,0:T(8,128)(2,1)}, u32[]{:S(2)}, u32[]{:S(2)}) async-start(bf16[8,9,64,512]{3,2,1,0:T(8,128)(2,1)} %stack.2), calls=%async_computation | async-start | bytes 9437184 | tf_op jit(solution)/shard_map/all_to_all | solution.py:51
  21.3 174.4 %all-gather.2.cloned.1.call-start = ((), (), s32[]{:S(2)}) async-start(), calls=%async_computation.1 | async-start | bytes 1769472 | tf_op jit(solution)/shard_map/all_gather | solution.py:57
  41.8 71.0 %copy-start.1 = (f32[512]{0:T(512)S(1)}, f32[512]{0:T(512)}, u32[]{:S(2)}) copy-start(f32[512]{0:T(512)} %param.8) | copy-start | bytes 6148
  112.8 108.3 %copy-start.2 = (f32[512]{0:T(512)S(1)}, f32[512]{0:T(512)}, u32[]{:S(2)}) copy-start(f32[512]{0:T(512)} %param.9) | copy-start | bytes 6148
  127.1 89.4 %collective-permute-start = (bf16[1,1,32,64,512]{4,3,2,1,0:T(8,128)(2,1)S(1)}, bf16[1,1,32,64,512]{4,3,2,1,0:T(8,128)(2,1)}, u32[]{:S(2)}, u32[]{:S(2)}) collective-permute-start(bf16[1,1,32,64,512]{4,3,2,1,0:T(8,128)(2,1)S(1)} %bitcast.13), channel_id=1, source_target_pairs={{0,1},{1,2},{2,3},{3,4},{4,5},{5,6},{6,7},{7,8},{8,9},{9,10},{10,1... | collective-permute-start | bytes 6291464 | tf_op jit(solution)/shard_map/ppermute | solution.py:12
  193.6 27.5 %collective-permute-start.1 = (bf16[1,1,32,64,512]{4,3,2,1,0:T(8,128)(2,1)S(1)}, bf16[1,1,32,64,512]{4,3,2,1,0:T(8,128)(2,1)}, u32[]{:S(2)}, u32[]{:S(2)}) collective-permute-start(bf16[1,1,32,64,512]{4,3,2,1,0:T(8,128)(2,1)S(1)} %bitcast.14), channel_id=1, source_target_pairs={{1,0},{2,1},{3,2},{4,3},{5,4},{6,5},{7,6},{8,7},{9,8},{10,9},{11,1... | collective-permute-start | bytes 6291464 | tf_op jit(solution)/shard_map/ppermute | solution.py:15
Sparse Core Ops, SparseCore 0:
  24.7 129.6 all-gather.1
